TPU v7x, 1024 devices: a whole 4x4x32 slice. The times are simulated.
1024 devices in a mesh: blk: 32 (over z_lo, core), uly: 32 (over y, x, z_hi).
Axes of the slice: x: 4, y: 4, z: 32 (z_hi: 2, z_lo: 16; z = z_hi * 16 + z_lo), core: 2. Of those that a mesh axis runs over, the one named last changes fastest.
Arguments:
- queries: bfloat16 [32768, 32, 128], P(('blk', 'uly')), may hold values from -6 to 6
- keys: bfloat16 [32768, 4, 128], P(('blk', 'uly')), may hold values from -6 to 6
- values: bfloat16 [32768, 4, 128], P(('blk', 'uly')), may hold values from -6 to 6
- grad_out: bfloat16 [32768, 32, 128], P(('blk', 'uly')), may hold values from -6 to 6
- stats: bfloat16 [32768, 32, 2], P(('blk', 'uly')), as said below
- placement: int32 [64], replicated, may hold values from 0 to 63, as said below
Outputs:
- grad_queries: bfloat16 [32768, 32, 128], P(('blk', 'uly'))
- key_accum: float32 [32768, 32, 128], P('blk', 'uly')
- value_accum: float32 [32768, 32, 128], P('blk', 'uly')
Inputs may be any that keep to these rules, and one draw needn't show every extreme that they name: `placement`: entries 2 b and 2 b + 1 are, in some order, r and 63 - r for some r < 32; each number of 0 to 63 appears once. `stats`: the first entry is the log of a softmax total of the forward pass; the second the row sum of the output gradient times the output.
All inputs are finite; a program needn't handle non-finite values.
Results may differ from a plain program's by a relative error of at most 0.007.
Values may be sent and summed in bfloat16 or wider, within the bound.
A program may use at most 32 MiB of HBM per device.

v0:
```python
import jax
import jax.numpy as jnp
from jax import lax
from jax.sharding import PartitionSpec as P


def passed_along(block, axis, distance):
    devices = range(lax.axis_size(axis))
    route = [((i - distance) % len(devices), i) for i in devices]
    return lax.ppermute(block, axis, route)


def block_grads(query_blk, grad_blk, stat_blk, key_blk, value_blk, query_pos, key_pos):
    factor = query_blk.shape[2] ** (-0.5)
    scores = (
        jnp.einsum("qhd,khd->hqk", query_blk, key_blk, preferred_element_type=jnp.float32) * factor
    )
    log_norm = stat_blk[:, :, 0].astype(jnp.float32).T[:, :, None]
    correction = stat_blk[:, :, 1].astype(jnp.float32).T[:, :, None]
    allowed = key_pos[None, :] <= query_pos[:, None]
    weights = jnp.where(allowed[None], jnp.exp(scores - log_norm), 0.0)
    grad_value = jnp.einsum(
        "hqk,qhd->khd", weights.astype(jnp.bfloat16), grad_blk, preferred_element_type=jnp.float32
    )
    grad_weights = jnp.einsum(
        "qhd,khd->hqk", grad_blk, value_blk, preferred_element_type=jnp.float32
    )
    grad_scores = (weights * (grad_weights - correction)).astype(jnp.bfloat16)
    grad_query = (
        jnp.einsum("hqk,khd->qhd", grad_scores, key_blk, preferred_element_type=jnp.float32)
        * factor
    )
    grad_key = (
        jnp.einsum("hqk,qhd->khd", grad_scores, query_blk, preferred_element_type=jnp.float32)
        * factor
    )
    return (grad_query, grad_key, grad_value)


def positions_of(placement, shard, piece_len):
    pieces = lax.dynamic_slice_in_dim(placement, 2 * shard, 2)
    return (pieces[:, None] * piece_len + jnp.arange(piece_len, dtype=jnp.int32)[None, :]).reshape(
        -1
    )


def per_device(queries, keys, values, grad_out, stats, placement):
    cycle_count = lax.axis_size("blk")
    shard = lax.axis_index("blk")
    repeats = queries.shape[1] // keys.shape[1]
    key_rep = jnp.repeat(keys, repeats, axis=1)
    value_rep = jnp.repeat(values, repeats, axis=1)
    query_heads, grad_heads, key_heads, value_heads, stat_heads = (
        lax.all_to_all(queries, "uly", split_axis=1, concat_axis=0, tiled=True),
        lax.all_to_all(grad_out, "uly", split_axis=1, concat_axis=0, tiled=True),
        lax.all_to_all(key_rep, "uly", split_axis=1, concat_axis=0, tiled=True),
        lax.all_to_all(value_rep, "uly", split_axis=1, concat_axis=0, tiled=True),
        lax.all_to_all(stats, "uly", split_axis=1, concat_axis=0, tiled=True),
    )
    key_before, value_before = passed_along((key_heads, value_heads), "blk", 1)
    piece_len = query_heads.shape[0] // 2
    previous = (shard - 1 + cycle_count) % cycle_count
    own_pos = positions_of(placement, shard, piece_len)
    prev_pos = positions_of(placement, previous, piece_len)
    query_first, key_first, value_first = block_grads(
        query_heads, grad_heads, stat_heads, key_heads, value_heads, own_pos, own_pos
    )
    key_arrived, value_arrived = (
        passed_along(key_first.astype(jnp.bfloat16), "blk", 1).astype(key_first.dtype),
        passed_along(value_first.astype(jnp.bfloat16), "blk", 1).astype(value_first.dtype),
    )
    query_second, key_second, value_second = block_grads(
        query_heads, grad_heads, stat_heads, key_before, value_before, own_pos, prev_pos
    )
    grad_query = (query_first + query_second).astype(jnp.bfloat16)
    grad_tokens = lax.all_to_all(grad_query, "uly", split_axis=0, concat_axis=1, tiled=True)
    return (grad_tokens, key_arrived + key_second, value_arrived + value_second)


def solution(mesh):
    in_specs = (
        P(("blk", "uly"), None, None),
        P(("blk", "uly"), None, None),
        P(("blk", "uly"), None, None),
        P(("blk", "uly"), None, None),
        P(("blk", "uly"), None, None),
        P(),
    )
    out_specs = (P(("blk", "uly"), None, None), P("blk", "uly", None), P("blk", "uly", None))
    return jax.shard_map(
        per_device, mesh=mesh, in_specs=in_specs, out_specs=out_specs, check_vma=False
    )
```

profile of v0, /device:TPU:2, one launch (start us, length us, event | category | flops | bytes accessed | tf_op | source)
XLA Modules:
  0.0 287.1 jit_solution(9640473763604343971)
XLA Ops:
  0.6 1.4 copy.42
  2.0 34.1 %all-to-all-start.2 = ((bf16[32,32,2]{0,2,1:T(2,128)(2,1)}), bf16[32,32,2]{0,2,1:T(2,128)(2,1)S(1)}, u32[]{:S(2)}, u32[]{:S(2)}) async-start(bf16[32,32,2]{0,2,1:T(2,128)(2,1)} %copy.42), calls=%async_computation.2 | async-start | bytes 32768 | tf_op jit(solution)/shard_map/all_to_all | solution.py:58
  36.2 1.8 copy.40
  37.9 23.5 %all-to-all-done.2 = bf16[32,32,2]{0,2,1:T(2,128)(2,1)S(1)} async-done(((bf16[32,32,2]{0,2,1:T(2,128)(2,1)}), bf16[32,32,2]{0,2,1:T(2,128)(2,1)S(1)}, u32[]{:S(2)}, u32[]{:S(2)}) %all-to-all-start.2) | async-done | bytes 4128 | tf_op jit(solution)/shard_map/all_to_all | solution.py:58
  61.4 5.0 %all-to-all-start = ((bf16[32,32,128]{2,0,1:T(8,128)(2,1)}), bf16[32,32,128]{2,0,1:T(8,128)(2,1)S(1)}, u32[]{:S(2)}, u32[]{:S(2)}) async-start(bf16[32,32,128]{2,0,1:T(8,128)(2,1)} %copy.40), calls=%async_computation | async-start | bytes 524288 | tf_op jit(solution)/shard_map/all_to_all | solution.py:54
  66.4 0.8 copy.41
  67.2 27.0 %all-to-all-done = bf16[32,32,128]{2,0,1:T(8,128)(2,1)S(1)} async-done(((bf16[32,32,128]{2,0,1:T(8,128)(2,1)}), bf16[32,32,128]{2,0,1:T(8,128)(2,1)S(1)}, u32[]{:S(2)}, u32[]{:S(2)}) %all-to-all-start) | async-done | bytes 262176 | tf_op jit(solution)/shard_map/all_to_all | solution.py:54
  95.0 5.0 %all-to-all-start.1 = ((bf16[32,32,128]{2,0,1:T(8,128)(2,1)}), bf16[32,32,128]{2,0,1:T(8,128)(2,1)S(1)}, u32[]{:S(2)}, u32[]{:S(2)}) async-start(bf16[32,32,128]{2,0,1:T(8,128)(2,1)} %bitcast.3), calls=%async_computation.1 | async-start | bytes 524288 | tf_op jit(solution)/shard_map/all_to_all | solution.py:56
  100.7 40.0 %all-to-all-done.1 = bf16[32,32,128]{2,0,1:T(8,128)(2,1)S(1)} async-done(((bf16[32,32,128]{2,0,1:T(8,128)(2,1)}), bf16[32,32,128]{2,0,1:T(8,128)(2,1)S(1)}, u32[]{:S(2)}, u32[]{:S(2)}) %all-to-all-start.1) | async-done | bytes 262176 | tf_op jit(solution)/shard_map/all_to_all | solution.py:56
  141.4 5.0 %all-to-all-start.4 = ((bf16[32,32,128]{2,0,1:T(8,128)(2,1)}), bf16[32,32,128]{2,0,1:T(8,128)(2,1)S(1)}, u32[]{:S(2)}, u32[]{:S(2)}) async-start(bf16[32,32,128]{2,0,1:T(8,128)(2,1)} %bitcast.13), calls=%async_computation.4 | async-start | bytes 524288 | tf_op jit(solution)/shard_map/all_to_all | solution.py:57
  146.4 1.8 copy.44
  148.1 25.3 %all-to-all-done.4 = bf16[32,32,128]{2,0,1:T(8,128)(2,1)S(1)} async-done(((bf16[32,32,128]{2,0,1:T(8,128)(2,1)}), bf16[32,32,128]{2,0,1:T(8,128)(2,1)S(1)}, u32[]{:S(2)}, u32[]{:S(2)}) %all-to-all-start.4) | async-done | bytes 262176 | tf_op jit(solution)/shard_map/all_to_all | solution.py:57
  173.4 5.0 %all-to-all-start.3 = ((bf16[32,32,128]{2,0,1:T(8,128)(2,1)}), bf16[32,32,128]{2,0,1:T(8,128)(2,1)S(1)}, u32[]{:S(2)}, u32[]{:S(2)}) async-start(bf16[32,32,128]{2,0,1:T(8,128)(2,1)} %copy.44), calls=%async_computation.3 | async-start | bytes 524288 | tf_op jit(solution)/shard_map/all_to_all | solution.py:55
  178.4 0.8 dynamic-slice_multiply_fusion
  179.4 1.9 collective-permute-start
  181.3 22.3 %collective-permute-start.1 = (bf16[1024,1,128]{2,0,1:T(8,128)(2,1)S(1)}, bf16[1024,1,128]{2,0,1:T(8,128)(2,1)S(1)}, u32[]{:S(2)}, u32[]{:S(2)}) collective-permute-start(bf16[1024,1,128]{2,0,1:T(8,128)(2,1)S(1)} %bitcast.118), channel_id=1, source_target_pairs={{992,0},{0,32},{32,64},{64,96},{96,128},{128,160},{160,192},{192,2... | collective-permute-start | bytes 786440 | tf_op jit(solution)/shard_map/ppermute | solution.py:10
  203.7 2.7 fusion.31
  206.3 3.2 %multiply_convert_fusion.1 = bf16[1024,1024]{1,0:T(8,128)(2,1)S(1)} fusion(f32[1024,1024]{1,0:T(8,128)} %fusion.31, bf16[1024,128]{1,0:T(8,128)(2,1)S(1)} %bitcast.114, bf16[1024,128]{1,0:T(8,128)(2,1)S(1)} %bitcast.119, f32[1024]{0:T(1024)S(1)} %bitcast.131, f32[1024]{0:T(1024)S(1)} %bitcast.127, s32[1024]{0:T(1024)S(1)} %bitcast.121), kind=kOutput, calls=%fused_computation.2 | convolution fusion | flops 275775488 | bytes 6828032 | tf_op jit(solution)/shard_map/qhd,khd->hqk/dot_general | solution.py:25
  210.9 12.1 %collective-permute-done = bf16[1024,1,128]{2,0,1:T(8,128)(2,1)S(1)} collective-permute-done((bf16[1024,1,128]{2,0,1:T(8,128)(2,1)S(1)}, bf16[1024,1,128]{2,0,1:T(8,128)(2,1)S(1)}, u32[]{:S(2)}, u32[]{:S(2)}) %collective-permute-start) | collective-permute-done | bytes 262176 | tf_op jit(solution)/shard_map/ppermute | solution.py:10
  223.7 2.1 collective-permute-done.1
  225.8 1.7 multiply_convert_fusion
  228.8 0.8 reduce
  230.4 12.7 %all-to-all-start.5 = ((bf16[32,2,2048]{2,1,0:T(2,128)(2,1)}), bf16[32,2,2048]{2,1,0:T(2,128)(2,1)S(1)}, u32[]{:S(2)}, u32[]{:S(2)}) async-start(bf16[32,2,2048]{2,1,0:T(2,128)(2,1)} %reshape.178), calls=%async_computation.5 | async-start | bytes 524288 | tf_op jit(solution)/shard_map/all_to_all | solution.py:76
  243.1 2.5 fusion.16
  245.6 1.9 collective-permute-start.2
  247.5 1.5 fusion.17
  249.0 3.7 %collective-permute-start.3 = (bf16[1024,1,128]{2,0,1:T(8,128)(2,1)S(1)}, bf16[1024,1,128]{2,0,1:T(8,128)(2,1)S(1)}, u32[]{:S(2)}, u32[]{:S(2)}) collective-permute-start(bf16[1024,1,128]{2,0,1:T(8,128)(2,1)S(1)} %fusion.17), channel_id=1, source_target_pairs={{992,0},{0,32},{32,64},{64,96},{96,128},{128,160},{160,192},{192,2... | collective-permute-start | bytes 786440 | tf_op jit(solution)/shard_map/ppermute | solution.py:10
  252.8 28.1 %collective-permute-done.2 = bf16[1024,1,128]{2,0,1:T(8,128)(2,1)S(1)} collective-permute-done((bf16[1024,1,128]{2,0,1:T(8,128)(2,1)S(1)}, bf16[1024,1,128]{2,0,1:T(8,128)(2,1)S(1)}, u32[]{:S(2)}, u32[]{:S(2)}) %collective-permute-start.2) | collective-permute-done | bytes 262176 | tf_op jit(solution)/shard_map/ppermute | solution.py:10
  280.9 1.5 convert_add_fusion.1
  282.4 1.3 collective-permute-done.3
  283.7 2.3 convert_add_fusion
  286.3 0.8 copy.47
  (26 shorter events, 6.8 us)
Async XLA Ops:
  2.0 59.4 %all-to-all-start.2 = ((bf16[32,32,2]{0,2,1:T(2,128)(2,1)}), bf16[32,32,2]{0,2,1:T(2,128)(2,1)S(1)}, u32[]{:S(2)}, u32[]{:S(2)}) async-start(bf16[32,32,2]{0,2,1:T(2,128)(2,1)} %copy.42), calls=%async_computation.2 | async-start | bytes 32768 | tf_op jit(solution)/shard_map/all_to_all | solution.py:58
  61.4 32.8 %all-to-all-start = ((bf16[32,32,128]{2,0,1:T(8,128)(2,1)}), bf16[32,32,128]{2,0,1:T(8,128)(2,1)S(1)}, u32[]{:S(2)}, u32[]{:S(2)}) async-start(bf16[32,32,128]{2,0,1:T(8,128)(2,1)} %copy.40), calls=%async_computation | async-start | bytes 524288 | tf_op jit(solution)/shard_map/all_to_all | solution.py:54
  95.0 45.7 %all-to-all-start.1 = ((bf16[32,32,128]{2,0,1:T(8,128)(2,1)}), bf16[32,32,128]{2,0,1:T(8,128)(2,1)S(1)}, u32[]{:S(2)}, u32[]{:S(2)}) async-start(bf16[32,32,128]{2,0,1:T(8,128)(2,1)} %bitcast.3), calls=%async_computation.1 | async-start | bytes 524288 | tf_op jit(solution)/shard_map/all_to_all | solution.py:56
  141.4 32.0 %all-to-all-start.4 = ((bf16[32,32,128]{2,0,1:T(8,128)(2,1)}), bf16[32,32,128]{2,0,1:T(8,128)(2,1)S(1)}, u32[]{:S(2)}, u32[]{:S(2)}) async-start(bf16[32,32,128]{2,0,1:T(8,128)(2,1)} %bitcast.13), calls=%async_computation.4 | async-start | bytes 524288 | tf_op jit(solution)/shard_map/all_to_all | solution.py:57
  173.4 32.9 %all-to-all-start.3 = ((bf16[32,32,128]{2,0,1:T(8,128)(2,1)}), bf16[32,32,128]{2,0,1:T(8,128)(2,1)S(1)}, u32[]{:S(2)}, u32[]{:S(2)}) async-start(bf16[32,32,128]{2,0,1:T(8,128)(2,1)} %copy.44), calls=%async_computation.3 | async-start | bytes 524288 | tf_op jit(solution)/shard_map/all_to_all | solution.py:55
  179.4 43.6 %collective-permute-start = (bf16[1024,1,128]{2,0,1:T(8,128)(2,1)S(1)}, bf16[1024,1,128]{2,0,1:T(8,128)(2,1)S(1)}, u32[]{:S(2)}, u32[]{:S(2)}) collective-permute-start(bf16[1024,1,128]{2,0,1:T(8,128)(2,1)S(1)} %bitcast.109), channel_id=1, source_target_pairs={{992,0},{0,32},{32,64},{64,96},{96,128},{128,160},{160,192},{192,2... | collective-permute-start | bytes 786440 | tf_op jit(solution)/shard_map/ppermute | solution.py:10
  181.3 44.5 %collective-permute-start.1 = (bf16[1024,1,128]{2,0,1:T(8,128)(2,1)S(1)}, bf16[1024,1,128]{2,0,1:T(8,128)(2,1)S(1)}, u32[]{:S(2)}, u32[]{:S(2)}) collective-permute-start(bf16[1024,1,128]{2,0,1:T(8,128)(2,1)S(1)} %bitcast.118), channel_id=1, source_target_pairs={{992,0},{0,32},{32,64},{64,96},{96,128},{128,160},{160,192},{192,2... | collective-permute-start | bytes 786440 | tf_op jit(solution)/shard_map/ppermute | solution.py:10
  209.5 1.4 copy-start.3
  223.7 3.8 %copy-start = (f32[1024,1024]{1,0:T(8,128)}, f32[1024,1024]{1,0:T(8,128)S(1)}, u32[]{:S(2)}) copy-start(f32[1024,1024]{1,0:T(8,128)S(1)} %fusion.23) | copy-start | bytes 12582916
  230.4 55.6 %all-to-all-start.5 = ((bf16[32,2,2048]{2,1,0:T(2,128)(2,1)}), bf16[32,2,2048]{2,1,0:T(2,128)(2,1)S(1)}, u32[]{:S(2)}, u32[]{:S(2)}) async-start(bf16[32,2,2048]{2,1,0:T(2,128)(2,1)} %reshape.178), calls=%async_computation.5 | async-start | bytes 524288 | tf_op jit(solution)/shard_map/all_to_all | solution.py:76
  243.0 4.4 %copy-start.2 = (f32[1024,1024]{1,0:T(8,128)S(1)}, f32[1024,1024]{1,0:T(8,128)}, u32[]{:S(2)}) copy-start(f32[1024,1024]{1,0:T(8,128)} %fusion.31) | copy-start | bytes 12582916
  245.6 35.3 %collective-permute-start.2 = (bf16[1024,1,128]{2,0,1:T(8,128)(2,1)S(1)}, bf16[1024,1,128]{2,0,1:T(8,128)(2,1)S(1)}, u32[]{:S(2)}, u32[]{:S(2)}) collective-permute-start(bf16[1024,1,128]{2,0,1:T(8,128)(2,1)S(1)} %fusion.16), channel_id=1, source_target_pairs={{992,0},{0,32},{32,64},{64,96},{96,128},{128,160},{160,192},{192,2... | collective-permute-start | bytes 786440 | tf_op jit(solution)/shard_map/ppermute | solution.py:10
  249.0 34.7 %copy-start.1 = (f32[1024,1024]{1,0:T(8,128)S(1)}, f32[1024,1024]{1,0:T(8,128)}, u32[]{:S(2)}) copy-start(f32[1024,1024]{1,0:T(8,128)} %copy-done) | copy-start | bytes 12582916
  249.0 34.7 %collective-permute-start.3 = (bf16[1024,1,128]{2,0,1:T(8,128)(2,1)S(1)}, bf16[1024,1,128]{2,0,1:T(8,128)(2,1)S(1)}, u32[]{:S(2)}, u32[]{:S(2)}) collective-permute-start(bf16[1024,1,128]{2,0,1:T(8,128)(2,1)S(1)} %fusion.17), channel_id=1, source_target_pairs={{992,0},{0,32},{32,64},{64,96},{96,128},{128,160},{160,192},{192,2... | collective-permute-start | bytes 786440 | tf_op jit(solution)/shard_map/ppermute | solution.py:10
where the time goes:
time: 288 us; the launch traced here: 287 us
  waiting for transfers between devices  159 us (55%)
  starting transfers between devices  96.6 us (34%)
  matrix products  17.5 us (6%)
  local copies, waits for them, and re-layouts  11.1 us (4%)
    ppermute x4, waiting for transfers between devices, passed_along(): return lax.ppermute(block, axis, route)  43.6 us
    all_to_all x1, waiting for transfers between devices, per_device(): lax.all_to_all(key_rep, 'uly', split_axis=1, concat_axis=0, tiled=True)  40 us
    all_to_all x1, starting transfers between devices, per_device(): lax.all_to_all(stats, 'uly', split_axis=1, concat_axis=0, tiled=True)  34.1 us
    ppermute x4, starting transfers between devices, passed_along(): return lax.ppermute(block, axis, route)  29.9 us
    all_to_all x1, waiting for transfers between devices, per_device(): lax.all_to_all(queries, 'uly', split_axis=1, concat_axis=0, tiled=True)  27 us
    all_to_all x1, waiting for transfers between devices, per_device(): lax.all_to_all(value_rep, 'uly', split_axis=1, concat_axis=0, tiled=True)  25.3 us
    all_to_all x1, waiting for transfers between devices, per_device(): lax.all_to_all(stats, 'uly', split_axis=1, concat_axis=0, tiled=True)  23.5 us
    all_to_all x1, starting transfers between devices, per_device(): lax.all_to_all(grad_query, 'uly', split_axis=0, concat_axis=1, tiled=True)  12.7 us
  transfers between devices with their start and end apart: 10, of which 8 were waited for; matrix products, arithmetic and copies ran while one was open for 7% of the time, Pallas kernels for 0%

commit v1 on v0

v1 whole, which is shorter than its diff:
```python
import functools

import jax
import jax.numpy as jnp
from jax import lax
from jax.experimental import pallas as pl
from jax.experimental.pallas import tpu as pltpu
from jax.sharding import PartitionSpec as P

MESH = pl.DeviceIdType.MESH
NT = (((1,), (1,)), ((), ()))
NN = (((1,), (0,)), ((), ()))
TN = (((0,), (0,)), ((), ()))


def dot(a, b, dims):
    return lax.dot_general(a, b, dims, preferred_element_type=jnp.float32)


def kernel(
    place, qin, gin, kvin, sin, dq_out, dk_out, dv_out,
    qbuf, gbuf, sbuf, kvbuf, acc, dqs, dkvs, dkvr,
    q_ss, q_rs, g_ss, g_rs, s_ss, s_rs, kv_ss, kv_rs, x_ss, x_rs, n_ss, n_rs,
    d_ss, d_rs, a_ss, a_rs, l_sem,
):
    f32, bf16 = jnp.float32, jnp.bfloat16
    blk, uly = lax.axis_index("blk"), lax.axis_index("uly")
    plane, half = uly // 2, uly % 2
    row, col = plane // 4, plane % 4
    nxt, prv = (blk + 1) % 32, (blk + 31) % 32
    kv_nxt = (nxt, plane * 2 + (half + (blk + 1) // 32) % 2)
    kv_prv = (prv, plane * 2 + (half + (32 - blk) // 32) % 2)
    factor = 128 ** (-0.5)

    def to(s):
        return ((plane + s % 16) % 16) * 2 + (half + s // 16) % 2

    def frm(s):
        return ((plane + 16 - s % 16) % 16) * 2 + (half + s // 16) % 2

    barrier = pltpu.get_barrier_semaphore()
    for s in range(1, 32):
        pl.semaphore_signal(barrier, inc=1, device_id=(blk, to(s)), device_id_type=MESH)
    for dev in (kv_nxt, kv_prv, (nxt, uly), (prv, uly)):
        pl.semaphore_signal(barrier, inc=1, device_id=dev, device_id_type=MESH)
    pl.semaphore_wait(barrier, 35)

    def remote(src, dst, ss, rs, dev):
        return pltpu.make_async_remote_copy(
            src_ref=src, dst_ref=dst, send_sem=ss, recv_sem=rs, device_id=dev, device_id_type=MESH
        )

    def kv_first(i):
        dest_row = (row + i % 4) % 4
        dest = (dest_row * 4 + col) * 2 + (half + i // 4) % 2
        return remote(
            kvin.at[:, dest_row], kvbuf.at[0, :, row, col, half], kv_ss.at[i], kv_rs.at[i],
            (blk, dest),
        )

    def kv_cols(slot, i):
        dest = (row * 4 + (col + i) % 4) * 2 + half
        return remote(
            kvbuf.at[slot, :, :, col], kvbuf.at[slot, :, :, col],
            x_ss.at[slot * 4 + i], x_rs.at[slot * 4 + i], (blk, dest),
        )

    kv_next = remote(kvbuf.at[0, :, :, col], kvbuf.at[1, :, :, col], n_ss.at[0], n_rs.at[0], kv_nxt)

    def stat_copy(s):
        return remote(sin.at[to(s)], sbuf.at[s], s_ss.at[s], s_rs.at[s], (blk, to(s)))

    def q_copy(s):
        return remote(qin.at[to(s)], qbuf.at[s], q_ss.at[s], q_rs.at[s], (blk, to(s)))

    def g_copy(s):
        return remote(gin.at[to(s)], gbuf.at[s], g_ss.at[s], g_rs.at[s], (blk, to(s)))

    def dq_copy(s):
        return remote(dqs.at[s], dq_out.at[uly], d_ss.at[s], d_rs.at[s], (blk, frm(s)))

    def dq_here(s):
        return remote(dqs.at[s], dq_out.at[to(s)], d_ss.at[s], d_rs.at[s], (blk, to(s)))

    for i in (4, 5, 6, 7, 1, 2, 3):
        kv_first(i).start()
    own_kv = pltpu.make_async_copy(kvin.at[:, row], kvbuf.at[0, :, row, col, half], l_sem.at[0])
    own_kv.start()
    for s in range(16):
        stat_copy(16 + s).start()
        q_copy(16 + s).start()
        g_copy(16 + s).start()
        if s:
            stat_copy(s).start()
            q_copy(s).start()
            g_copy(s).start()
    qbuf[0] = qin[uly]
    gbuf[0] = gin[uly]
    sbuf[0] = sin[uly]
    acc[...] = jnp.zeros_like(acc)

    own_kv.wait()
    for i in (1, 2, 3, 4, 5, 6, 7):
        kv_first(i).wait_recv()
    kv_next.start()
    for i in (1, 2, 3):
        kv_cols(0, i).start()
    kv_next.wait_recv()
    for i in (1, 2, 3):
        kv_cols(1, i).start()
    for slot in (0, 1):
        for i in (1, 2, 3):
            kv_cols(slot, i).wait_recv()

    lane = lax.broadcasted_iota(jnp.int32, (1, 128), 1)
    lane2 = lax.broadcasted_iota(jnp.int32, (2, 128), 1)
    krow = lax.broadcasted_iota(jnp.int32, (512, 1), 0)

    def chunk(c):
        base = 4 * c
        st = jnp.zeros((2, 128), f32)
        for j in range(4):
            st = jnp.where(lane2 // 32 == j, sbuf[base + j], st)
        lse, corr = st[0:1], st[1:2]
        src = ((plane + 16 - (base % 16) - lane // 32) % 16) * 2 + (half + c // 4) % 2
        place_q = jnp.where(src >= 16, place[2 * blk + 1], place[2 * blk])
        qpos = place_q * 512 + (src % 16) * 32 + lane % 32
        q = qbuf[pl.ds(base, 4)].reshape(128, 128)
        g = gbuf[pl.ds(base, 4)].reshape(128, 128)

        def tile(t, dq):
            slot, part = t // 2, t % 2
            kblk = (blk + 32 - slot) % 32
            k = kvbuf[slot, 0, pl.ds(2 * part, 2)].reshape(512, 128)
            v = kvbuf[slot, 1, pl.ds(2 * part, 2)].reshape(512, 128)
            kpos = place[2 * kblk + part] * 512 + krow
            scores = dot(k, q, NT) * factor - lse
            weights = jnp.where(kpos <= qpos, jnp.exp(scores), 0.0)
            dweights = dot(v, g, NT)
            dscores = (weights * (dweights - corr)).astype(bf16)
            acc[t, 1] += dot(weights.astype(bf16), g, NN)
            acc[t, 0] += dot(dscores, q, NN)
            return dq + dot(dscores, k, TN)

        dq = lax.fori_loop(0, 4, tile, jnp.zeros((128, 128), f32))
        dqs[pl.ds(base, 4)] = (dq * factor).astype(bf16).reshape(4, 32, 128)

    def arrive(s):
        stat_copy(s).wait_recv()
        q_copy(s).wait_recv()
        g_copy(s).wait_recv()

    for s in (1, 2, 3):
        arrive(s)
    chunk(0)
    dq_out[uly] = dqs[0]
    for s in (1, 2, 3):
        dq_copy(s).start()

    def step(c, carry):
        for j in range(4):
            arrive(4 * c + j)
        chunk(c)
        for j in range(4):
            dq_copy(4 * c + j).start()
        return carry

    lax.fori_loop(1, 8, step, 0)

    for part in range(2):
        for a in range(2):
            scale = 1.0 if a else factor
            dkvs[a, pl.ds(part * 512, 512)] = (acc[part, a] * scale).astype(bf16)
    accum = [
        remote(dkvs.at[a], dkvr.at[a], a_ss.at[a], a_rs.at[a], (nxt, uly)) for a in range(2)
    ]
    for copy in accum:
        copy.start()
    for a, out in ((0, dk_out), (1, dv_out)):
        accum[a].wait_recv()
        for part in range(2):
            scale = 1.0 if a else factor
            rows = pl.ds(part * 512, 512)
            out[rows] = acc[2 + part, a] * scale + dkvr[a, rows].astype(f32)

    def drain(s, carry):
        dq_here(s).wait_recv()
        dq_copy(s).wait_send()
        stat_copy(s).wait_send()
        q_copy(s).wait_send()
        g_copy(s).wait_send()
        return carry

    lax.fori_loop(1, 32, drain, 0)
    for i in range(1, 8):
        kv_first(i).wait_send()
    kv_next.wait_send()
    for slot in (0, 1):
        for i in (1, 2, 3):
            kv_cols(slot, i).wait_send()
    for copy in accum:
        copy.wait_send()


def per_device(queries, keys, values, grad_out, stats, placement):
    f32, bf16 = jnp.float32, jnp.bfloat16
    q_heads = queries.transpose(1, 0, 2)
    g_heads = grad_out.transpose(1, 0, 2)
    kv_heads = jnp.stack([keys.transpose(1, 0, 2), values.transpose(1, 0, 2)])
    stat_rows = jnp.tile(stats.transpose(1, 2, 0).astype(f32), (1, 1, 4))
    vmem = pl.BlockSpec(memory_space=pltpu.VMEM)
    sem = pltpu.SemaphoreType.DMA
    dq, dk, dv = pl.pallas_call(
        kernel,
        name="exchange_grads",
        out_shape=(
            jax.ShapeDtypeStruct((32, 32, 128), bf16),
            jax.ShapeDtypeStruct((1024, 128), f32),
            jax.ShapeDtypeStruct((1024, 128), f32),
        ),
        in_specs=[pl.BlockSpec(memory_space=pltpu.SMEM)] + [vmem] * 4,
        out_specs=(vmem, vmem, vmem),
        scratch_shapes=[
            pltpu.VMEM((32, 32, 128), bf16),
            pltpu.VMEM((32, 32, 128), bf16),
            pltpu.VMEM((32, 2, 128), f32),
            pltpu.VMEM((2, 2, 4, 4, 2, 32, 128), bf16),
            pltpu.VMEM((4, 2, 512, 128), f32),
            pltpu.VMEM((32, 32, 128), bf16),
            pltpu.VMEM((2, 1024, 128), bf16),
            pltpu.VMEM((2, 1024, 128), bf16),
            sem((32,)), sem((32,)), sem((32,)), sem((32,)), sem((32,)), sem((32,)),
            sem((8,)), sem((8,)), sem((8,)), sem((8,)), sem((1,)), sem((1,)),
            sem((32,)), sem((32,)), sem((2,)), sem((2,)), sem((1,)),
        ],
        compiler_params=pltpu.CompilerParams(collective_id=0, has_side_effects=True),
    )(placement, q_heads, g_heads, kv_heads, stat_rows)
    return dq.transpose(1, 0, 2), dk[:, None, :], dv[:, None, :]


def solution(mesh):
    tokens = P(("blk", "uly"), None, None)
    return jax.shard_map(
        per_device,
        mesh=mesh,
        in_specs=(tokens,) * 5 + (P(),),
        out_specs=(tokens, P("blk", "uly", None), P("blk", "uly", None)),
        check_vma=False,
    )
```

time: 288 us -> 152 us (0.53)
  the two profiles are of different devices: /device:TPU:2 before, /device:TPU:32 now
where the time goes in v1:
time: 152 us
  Pallas kernels  144 us (95%)
  local copies, waits for them, and re-layouts  6.39 us (4%)
    pallas_call x1, Pallas kernels, per_device(): pl.pallas_call(kernel, name='exchange_grads', out_shape=(jax.ShapeDtypeSt...  144 us
    unnamed x15, local copies, waits for them, and re-layouts  4.53 us

profile of v1, /device:TPU:32, one launch (start us, length us, event | category | flops | bytes accessed | tf_op | source)
XLA Modules:
  0.0 152.0 jit_solution(11444467533409002160)
XLA Ops:
  0.6 0.7 convert_bitcast_fusion
  1.4 0.0 copy-start.4
  1.4 0.0 copy-start.5
  1.4 0.1 copy.13
  1.5 0.7 copy-done.4
  2.1 0.0 copy-done.5
  2.1 0.0 copy-start.3
  2.2 0.0 copy-start.2
  2.2 0.6 pad_maximum_fusion.kvin
  2.8 0.7 tile.10.sin
  3.6 0.0 copy-done.3
  3.6 0.0 copy-done.2
  3.6 1.0 copy_bitcast_fusion
  4.6 143.6 %exchange_grads.1 = (bf16[32,32,128]{2,1,0:T(8,128)(2,1)}, f32[1024,128]{1,0:T(8,128)}, f32[1024,128]{1,0:T(8,128)}) custom-call(s32[64]{0:T(128)} %place.1, bf16[32,32,128]{2,1,0:T(8,128)(2,1)} %get-tuple-element.15.qin, bf16[32,32,128]{2,1,0:T(8,128)(2,1)} %get-tuple-element.14.gin, bf16[2,4,32,128]{3,2,1,0:T(8,128)(2,1)} %pad_maximum_fusion.kvin, ...), custom_call_target="tpu_custom_call" | custom-call | tf_op jit(solution)/shard_map/exchange_grads/pallas_call | solution.py:213
  148.2 0.0 copy-start.1
  148.2 1.8 %copy.14 = bf16[32,32,128]{2,1,0:T(8,128)(2,1)} copy(bf16[32,32,128]{2,0,1:T(8,128)(2,1)} %bitcast.23) | data formatting | bytes 524288
  150.0 0.0 copy-done.1
  150.0 0.0 copy-start
  150.0 0.8 copy.23
  150.8 0.4 copy-done
  151.2 0.8 copy.24
  (2 shorter events, 0.0 us)
Async XLA Ops:
  1.4 0.8 copy-start.4
  1.4 0.8 copy-start.5
  2.1 1.4 copy-start.3
  2.2 1.4 copy-start.2
  148.2 1.8 %copy-start.1 = (f32[1024,128]{1,0:T(8,128)S(1)}, f32[1024,128]{1,0:T(8,128)}, u32[]{:S(2)}) copy-start(f32[1024,128]{1,0:T(8,128)} %get-tuple-element.7) | copy-start | bytes 1572868
  150.0 1.2 copy-start

commit v2 on v1

--- a/solution.py
+++ b/solution.py
@@ -1,5 +1,3 @@
-import functools
-
 import jax
 import jax.numpy as jnp
 from jax import lax
@@ -18,9 +16,9 @@
 
 
 def kernel(
-    place, qin, gin, kvin, sin, dq_out, dk_out, dv_out,
-    qbuf, gbuf, sbuf, kvbuf, acc, dqs, dkvs, dkvr,
-    q_ss, q_rs, g_ss, g_rs, s_ss, s_rs, kv_ss, kv_rs, x_ss, x_rs, n_ss, n_rs,
+    place, qin, gin, kin, vin, sin, dq_out, dk_out, dv_out,
+    qgs, qgbuf, kvin, sbuf, kvbuf, acc, dqs, dkvs, dkvr,
+    q_ss, q_rs, s_ss, s_rs, kv_ss, kv_rs, x_ss, x_rs, n_ss, n_rs,
     d_ss, d_rs, a_ss, a_rs, l_sem,
 ):
     f32, bf16 = jnp.float32, jnp.bfloat16
@@ -43,6 +41,11 @@
         pl.semaphore_signal(barrier, inc=1, device_id=(blk, to(s)), device_id_type=MESH)
     for dev in (kv_nxt, kv_prv, (nxt, uly), (prv, uly)):
         pl.semaphore_signal(barrier, inc=1, device_id=dev, device_id_type=MESH)
+    kvin[0] = kin[...].transpose(1, 0, 2)
+    kvin[1] = vin[...].transpose(1, 0, 2)
+    qgs[:, 0] = qin[...].transpose(1, 0, 2)
+    qgs[:, 1] = gin[...].transpose(1, 0, 2)
+    acc[...] = jnp.zeros_like(acc)
     pl.semaphore_wait(barrier, 35)
 
     def remote(src, dst, ss, rs, dev):
@@ -70,11 +73,8 @@
     def stat_copy(s):
         return remote(sin.at[to(s)], sbuf.at[s], s_ss.at[s], s_rs.at[s], (blk, to(s)))
 
-    def q_copy(s):
-        return remote(qin.at[to(s)], qbuf.at[s], q_ss.at[s], q_rs.at[s], (blk, to(s)))
-
-    def g_copy(s):
-        return remote(gin.at[to(s)], gbuf.at[s], g_ss.at[s], g_rs.at[s], (blk, to(s)))
+    def qg_copy(s):
+        return remote(qgs.at[to(s)], qgbuf.at[s], q_ss.at[s], q_rs.at[s], (blk, to(s)))
 
     def dq_copy(s):
         return remote(dqs.at[s], dq_out.at[uly], d_ss.at[s], d_rs.at[s], (blk, frm(s)))
@@ -86,18 +86,15 @@
         kv_first(i).start()
     own_kv = pltpu.make_async_copy(kvin.at[:, row], kvbuf.at[0, :, row, col, half], l_sem.at[0])
     own_kv.start()
-    for s in range(16):
-        stat_copy(16 + s).start()
-        q_copy(16 + s).start()
-        g_copy(16 + s).start()
-        if s:
+    def send(lo, hi):
+        for s in range(lo, hi):
             stat_copy(s).start()
-            q_copy(s).start()
-            g_copy(s).start()
-    qbuf[0] = qin[uly]
-    gbuf[0] = gin[uly]
+            qg_copy(s).start()
+
+    send(16, 20)
+    send(1, 16)
+    qgbuf[0] = qgs[uly]
     sbuf[0] = sin[uly]
-    acc[...] = jnp.zeros_like(acc)
 
     own_kv.wait()
     for i in (1, 2, 3, 4, 5, 6, 7):
@@ -105,9 +102,11 @@
     kv_next.start()
     for i in (1, 2, 3):
         kv_cols(0, i).start()
+    send(20, 24)
     kv_next.wait_recv()
     for i in (1, 2, 3):
         kv_cols(1, i).start()
+    send(24, 32)
     for slot in (0, 1):
         for i in (1, 2, 3):
             kv_cols(slot, i).wait_recv()
@@ -125,8 +124,8 @@
         src = ((plane + 16 - (base % 16) - lane // 32) % 16) * 2 + (half + c // 4) % 2
         place_q = jnp.where(src >= 16, place[2 * blk + 1], place[2 * blk])
         qpos = place_q * 512 + (src % 16) * 32 + lane % 32
-        q = qbuf[pl.ds(base, 4)].reshape(128, 128)
-        g = gbuf[pl.ds(base, 4)].reshape(128, 128)
+        q = qgbuf[pl.ds(base, 4), 0].reshape(128, 128)
+        g = qgbuf[pl.ds(base, 4), 1].reshape(128, 128)
 
         def tile(t, dq):
             slot, part = t // 2, t % 2
@@ -147,8 +146,7 @@
 
     def arrive(s):
         stat_copy(s).wait_recv()
-        q_copy(s).wait_recv()
-        g_copy(s).wait_recv()
+        qg_copy(s).wait_recv()
 
     for s in (1, 2, 3):
         arrive(s)
@@ -187,8 +185,7 @@
         dq_here(s).wait_recv()
         dq_copy(s).wait_send()
         stat_copy(s).wait_send()
-        q_copy(s).wait_send()
-        g_copy(s).wait_send()
+        qg_copy(s).wait_send()
         return carry
 
     lax.fori_loop(1, 32, drain, 0)
@@ -204,9 +201,6 @@
 
 def per_device(queries, keys, values, grad_out, stats, placement):
     f32, bf16 = jnp.float32, jnp.bfloat16
-    q_heads = queries.transpose(1, 0, 2)
-    g_heads = grad_out.transpose(1, 0, 2)
-    kv_heads = jnp.stack([keys.transpose(1, 0, 2), values.transpose(1, 0, 2)])
     stat_rows = jnp.tile(stats.transpose(1, 2, 0).astype(f32), (1, 1, 4))
     vmem = pl.BlockSpec(memory_space=pltpu.VMEM)
     sem = pltpu.SemaphoreType.DMA
@@ -218,23 +212,24 @@
             jax.ShapeDtypeStruct((1024, 128), f32),
             jax.ShapeDtypeStruct((1024, 128), f32),
         ),
-        in_specs=[pl.BlockSpec(memory_space=pltpu.SMEM)] + [vmem] * 4,
+        in_specs=[pl.BlockSpec(memory_space=pltpu.SMEM)] + [vmem] * 5,
         out_specs=(vmem, vmem, vmem),
         scratch_shapes=[
-            pltpu.VMEM((32, 32, 128), bf16),
-            pltpu.VMEM((32, 32, 128), bf16),
+            pltpu.VMEM((32, 2, 32, 128), bf16),
+            pltpu.VMEM((32, 2, 32, 128), bf16),
+            pltpu.VMEM((2, 4, 32, 128), bf16),
             pltpu.VMEM((32, 2, 128), f32),
             pltpu.VMEM((2, 2, 4, 4, 2, 32, 128), bf16),
             pltpu.VMEM((4, 2, 512, 128), f32),
             pltpu.VMEM((32, 32, 128), bf16),
             pltpu.VMEM((2, 1024, 128), bf16),
             pltpu.VMEM((2, 1024, 128), bf16),
-            sem((32,)), sem((32,)), sem((32,)), sem((32,)), sem((32,)), sem((32,)),
+            sem((32,)), sem((32,)), sem((32,)), sem((32,)),
             sem((8,)), sem((8,)), sem((8,)), sem((8,)), sem((1,)), sem((1,)),
             sem((32,)), sem((32,)), sem((2,)), sem((2,)), sem((1,)),
         ],
         compiler_params=pltpu.CompilerParams(collective_id=0, has_side_effects=True),
-    )(placement, q_heads, g_heads, kv_heads, stat_rows)
+    )(placement, queries, grad_out, keys, values, stat_rows)
     return dq.transpose(1, 0, 2), dk[:, None, :], dv[:, None, :]
 
 

time: 152 us -> 150 us (0.987)
  local copies, waits for them, and re-layouts: 6.39 us -> 4.7 us
    unnamed x15 -> x7, local copies, waits for them, and re-layouts: 4.53 us -> 3.84 us
where the time goes in v2:
time: 150 us
  Pallas kernels  144 us (96%)
  local copies, waits for them, and re-layouts  4.7 us (3%)
    pallas_call x1, Pallas kernels, per_device(): pl.pallas_call(kernel, name='exchange_grads', out_shape=(jax.ShapeDtypeSt...  144 us
    unnamed x7, local copies, waits for them, and re-layouts  3.84 us

profile of v2, /device:TPU:32, one launch (start us, length us, event | category | flops | bytes accessed | tf_op | source)
XLA Modules:
  0.0 150.2 jit_solution(1802012650204012699)
XLA Ops:
  0.6 0.7 convert_bitcast_fusion
  1.4 0.1 copy.9
  1.5 0.8 tile.10.sin
  2.2 144.1 %exchange_grads.1 = (bf16[32,32,128]{2,1,0:T(8,128)(2,1)}, f32[1024,128]{1,0:T(8,128)}, f32[1024,128]{1,0:T(8,128)}) custom-call(s32[64]{0:T(128)} %place.1, bf16[32,32,128]{2,1,0:T(8,128)(2,1)} %qin.1, bf16[32,32,128]{2,1,0:T(8,128)(2,1)} %gin.1, bf16[32,4,128]{2,1,0:T(4,128)(2,1)} %kin.1, bf16[32,4,128]{2,1,0:T(4,128)(2,1)} %vin.1, f32[32,2,128]{2,1,0:T(2,128)} %tile.10.sin), custom_call_target="tpu_custom_call" | custom-call | tf_op jit(solution)/shard_map/exchange_grads/pallas_call | solution.py:207
  146.3 0.0 copy-start.1
  146.3 1.8 %copy.10 = bf16[32,32,128]{2,1,0:T(8,128)(2,1)} copy(bf16[32,32,128]{2,0,1:T(8,128)(2,1)} %bitcast.11) | data formatting | bytes 524288
  148.2 0.0 copy-done.1
  148.2 0.0 copy-start
  148.2 0.8 copy.15
  149.0 0.4 copy-done
  149.4 0.8 copy.16
  (1 shorter events, 0.0 us)
Async XLA Ops:
  146.3 1.8 %copy-start.1 = (f32[1024,128]{1,0:T(8,128)S(1)}, f32[1024,128]{1,0:T(8,128)}, u32[]{:S(2)}) copy-start(f32[1024,128]{1,0:T(8,128)} %get-tuple-element.7) | copy-start | bytes 1572868
  148.2 1.2 copy-start

commit v3 on v2

v3 whole, which is shorter than its diff:
```python
import jax
import jax.numpy as jnp
from jax import lax
from jax.experimental import pallas as pl
from jax.experimental.pallas import tpu as pltpu
from jax.sharding import PartitionSpec as P

MESH = pl.DeviceIdType.MESH
NT = (((1,), (1,)), ((), ()))
NN = (((1,), (0,)), ((), ()))
TN = (((0,), (0,)), ((), ()))


def dot(a, b, dims):
    return lax.dot_general(a, b, dims, preferred_element_type=jnp.float32)


def kernel(
    place, qin, gin, kin, vin, sin, dq_out, dk_out, dv_out,
    qgs, inbuf, crossbuf, kvin, sinbuf, scross, kvbuf, acc, dqs, dqx, dkvs, dkvr,
    q_ss, q_rs, s_ss, s_rs, c_ss, c_rs, t_ss, t_rs, kv_ss, kv_rs, x_ss, x_rs, n_ss, n_rs,
    d_ss, d_rs, y_ss, y_rs, f_ss, f_rs, a_ss, a_rs, l_sem,
):
    f32, bf16 = jnp.float32, jnp.bfloat16
    blk, uly = lax.axis_index("blk"), lax.axis_index("uly")
    plane, half = uly // 2, uly % 2
    row, col = plane // 4, plane % 4
    nxt, prv = (blk + 1) % 32, (blk + 31) % 32
    kv_nxt = (nxt, plane * 2 + (half + (blk + 1) // 32) % 2)
    kv_prv = (prv, plane * 2 + (half + (32 - blk) // 32) % 2)
    factor = 128 ** (-0.5)

    def to(s):
        return ((plane + s % 16) % 16) * 2 + (half + s // 16) % 2

    def frm(s):
        return ((plane + 16 - s % 16) % 16) * 2 + (half + s // 16) % 2

    barrier = pltpu.get_barrier_semaphore()
    for s in tuple(range(1, 17)) + (20, 24, 28):
        pl.semaphore_signal(barrier, inc=1, device_id=(blk, to(s)), device_id_type=MESH)
    for dev in (kv_nxt, kv_prv, (nxt, uly), (prv, uly)):
        pl.semaphore_signal(barrier, inc=1, device_id=dev, device_id_type=MESH)
    kvin[0] = kin[...].transpose(1, 0, 2)
    kvin[1] = vin[...].transpose(1, 0, 2)
    qgs[:, 0] = qin[...].transpose(1, 0, 2)
    qgs[:, 1] = gin[...].transpose(1, 0, 2)
    acc[...] = jnp.zeros_like(acc)
    pl.semaphore_wait(barrier, 23)

    def remote(src, dst, ss, rs, dev):
        return pltpu.make_async_remote_copy(
            src_ref=src, dst_ref=dst, send_sem=ss, recv_sem=rs, device_id=dev, device_id_type=MESH
        )

    def kv_first(i):
        dest_row = (row + i % 4) % 4
        dest = (dest_row * 4 + col) * 2 + (half + i // 4) % 2
        return remote(
            kvin.at[:, dest_row], kvbuf.at[0, :, row, col, half], kv_ss.at[i], kv_rs.at[i],
            (blk, dest),
        )

    def kv_cols(slot, i):
        dest = (row * 4 + (col + i) % 4) * 2 + half
        return remote(
            kvbuf.at[slot, :, :, col], kvbuf.at[slot, :, :, col],
            x_ss.at[slot * 4 + i], x_rs.at[slot * 4 + i], (blk, dest),
        )

    kv_next = remote(kvbuf.at[0, :, :, col], kvbuf.at[1, :, :, col], n_ss.at[0], n_rs.at[0], kv_nxt)

    far = plane * 2 + (half + 1) % 2

    def pair(r):
        return pl.ds(((plane + r) % 16) * 2, 2)

    def stat_plane(r):
        return remote(sin.at[pair(r)], sinbuf.at[:, r], s_ss.at[r], s_rs.at[r], (blk, to(r)))

    def qg_plane(r):
        return remote(qgs.at[pair(r)], inbuf.at[:, r], q_ss.at[r], q_rs.at[r], (blk, to(r)))

    def stat_cross(c):
        rows = pl.ds(4 * c, 4)
        return remote(
            sinbuf.at[1 - half, rows], scross.at[rows], t_ss.at[c], t_rs.at[c], (blk, far)
        )

    def qg_cross(c):
        rows = pl.ds(4 * c, 4)
        return remote(
            inbuf.at[1 - half, rows], crossbuf.at[rows], c_ss.at[c], c_rs.at[c], (blk, far)
        )

    def dq_plane(r):
        return remote(dqs.at[r], dq_out.at[uly], d_ss.at[r], d_rs.at[r], (blk, frm(r)))

    def dq_here(r):
        return remote(dqs.at[r], dq_out.at[to(r)], d_ss.at[r], d_rs.at[r], (blk, to(r)))

    def dq_cross(c):
        rows = pl.ds(4 * c, 4)
        return remote(
            dqs.at[pl.ds(16 + 4 * c, 4)], dqx.at[rows], y_ss.at[c], y_rs.at[c], (blk, far)
        )

    def dq_pass(r):
        return remote(dqx.at[r], dq_out.at[far], f_ss.at[r], f_rs.at[r], (blk, frm(r)))

    def dq_passed(r):
        head = ((plane + r) % 16) * 2 + 1 - half
        return remote(dqx.at[r], dq_out.at[head], f_ss.at[r], f_rs.at[r], (blk, to(r)))

    for i in (4, 5, 6, 7, 1, 2, 3):
        kv_first(i).start()
    own_kv = pltpu.make_async_copy(kvin.at[:, row], kvbuf.at[0, :, row, col, half], l_sem.at[0])
    own_kv.start()
    own_qg = pltpu.make_async_copy(qgs.at[pair(0)], inbuf.at[:, 0], l_sem.at[1])
    own_qg.start()
    own_stat = pltpu.make_async_copy(sin.at[pair(0)], sinbuf.at[:, 0], l_sem.at[2])
    own_stat.start()
    for r in range(1, 16):
        stat_plane(r).start()
        qg_plane(r).start()

    def cross(c):
        if c == 0:
            own_qg.wait()
            own_stat.wait()
        for r in range(max(1, 4 * c), 4 * c + 4):
            stat_plane(r).wait_recv()
            qg_plane(r).wait_recv()
        stat_cross(c).start()
        qg_cross(c).start()

    cross(0)
    cross(1)
    own_kv.wait()
    for i in (1, 2, 3, 4, 5, 6, 7):
        kv_first(i).wait_recv()
    kv_next.start()
    for i in (1, 2, 3):
        kv_cols(0, i).start()
    cross(2)
    kv_next.wait_recv()
    for i in (1, 2, 3):
        kv_cols(1, i).start()
    cross(3)
    for slot in (0, 1):
        for i in (1, 2, 3):
            kv_cols(slot, i).wait_recv()

    lane = lax.broadcasted_iota(jnp.int32, (1, 128), 1)
    krow = lax.broadcasted_iota(jnp.int32, (1024, 1), 0)

    def chunk(c, stats, qg):
        base = 4 * c
        lse = corr = jnp.zeros((1, 128), f32)
        for j in range(4):
            here = stats(j)
            turned = pltpu.roll(here, 32, 1)
            first, second = (here, turned) if j % 2 == 0 else (turned, here)
            lse = jnp.where(lane // 32 == j, first, lse)
            corr = jnp.where(lane // 32 == j, second, corr)
        src = ((plane + 16 - (base % 16) - lane // 32) % 16) * 2 + (half + c // 4) % 2
        place_q = jnp.where(src >= 16, place[2 * blk + 1], place[2 * blk])
        qpos = place_q * 512 + (src % 16) * 32 + lane % 32
        q, g = qg(0).reshape(128, 128), qg(1).reshape(128, 128)

        def tile(slot, dq):
            kblk = (blk + 32 - slot) % 32
            k = kvbuf[slot, 0].reshape(1024, 128)
            v = kvbuf[slot, 1].reshape(1024, 128)
            place_k = jnp.where(krow >= 512, place[2 * kblk + 1], place[2 * kblk])
            kpos = place_k * 512 + krow % 512
            scores = dot(k, q, NT) * factor - lse
            weights = jnp.where(kpos <= qpos, jnp.exp(scores), 0.0)
            dweights = dot(v, g, NT)
            dscores = (weights * (dweights - corr)).astype(bf16)
            acc[slot, 1] += dot(weights.astype(bf16), g, NN)
            acc[slot, 0] += dot(dscores, q, NN)
            return dq + dot(dscores, k, TN)

        dq = lax.fori_loop(0, 2, tile, jnp.zeros((128, 128), f32))
        dqs[pl.ds(base, 4)] = (dq * factor).astype(bf16).reshape(4, 32, 128)

    def near_chunk(c):
        chunk(
            c,
            lambda j: sinbuf[half, 4 * c + j],
            lambda a: inbuf[half, pl.ds(4 * c, 4), a],
        )

    near_chunk(0)
    dq_out[uly] = dqs[0]
    for r in (1, 2, 3):
        dq_plane(r).start()

    def near(c, carry):
        near_chunk(c)
        for j in range(4):
            dq_plane(4 * c + j).start()
        return carry

    lax.fori_loop(1, 4, near, 0)

    def distant(c, carry):
        stat_cross(c).wait_recv()
        qg_cross(c).wait_recv()
        chunk(
            c + 4,
            lambda j: scross[4 * c + j],
            lambda a: crossbuf[pl.ds(4 * c, 4), a],
        )
        dq_cross(c).start()
        return carry

    lax.fori_loop(0, 4, distant, 0)

    dkvs[0] = (acc[0, 0] * factor).astype(bf16)
    dkvs[1] = acc[0, 1].astype(bf16)
    accum = [
        remote(dkvs.at[a], dkvr.at[a], a_ss.at[a], a_rs.at[a], (nxt, uly)) for a in range(2)
    ]
    for copy in accum:
        copy.start()
    dq_cross(0).wait_recv()
    dq_out[far] = dqx[0]
    for r in (1, 2, 3):
        dq_pass(r).start()

    def onward(c, carry):
        dq_cross(c).wait_recv()
        for j in range(4):
            dq_pass(4 * c + j).start()
        return carry

    lax.fori_loop(1, 4, onward, 0)
    for a, out in ((0, dk_out), (1, dv_out)):
        accum[a].wait_recv()
        out[...] = acc[1, a] * (1.0 if a else factor) + dkvr[a].astype(f32)

    def drain(r, carry):
        dq_here(r).wait_recv()
        dq_passed(r).wait_recv()
        dq_plane(r).wait_send()
        dq_pass(r).wait_send()
        stat_plane(r).wait_send()
        qg_plane(r).wait_send()
        return carry

    lax.fori_loop(1, 16, drain, 0)
    for c in range(4):
        stat_cross(c).wait_send()
        qg_cross(c).wait_send()
        dq_cross(c).wait_send()
    for i in range(1, 8):
        kv_first(i).wait_send()
    kv_next.wait_send()
    for slot in (0, 1):
        for i in (1, 2, 3):
            kv_cols(slot, i).wait_send()
    for copy in accum:
        copy.wait_send()


def per_device(queries, keys, values, grad_out, stats, placement):
    f32, bf16 = jnp.float32, jnp.bfloat16
    stat_rows = jnp.tile(stats.transpose(1, 2, 0).astype(f32).reshape(32, 1, 64), (1, 1, 2))
    vmem = pl.BlockSpec(memory_space=pltpu.VMEM)
    sem = pltpu.SemaphoreType.DMA
    dq, dk, dv = pl.pallas_call(
        kernel,
        name="exchange_grads",
        out_shape=(
            jax.ShapeDtypeStruct((32, 32, 128), bf16),
            jax.ShapeDtypeStruct((1024, 128), f32),
            jax.ShapeDtypeStruct((1024, 128), f32),
        ),
        in_specs=[pl.BlockSpec(memory_space=pltpu.SMEM)] + [vmem] * 5,
        out_specs=(vmem, vmem, vmem),
        scratch_shapes=[
            pltpu.VMEM((32, 2, 32, 128), bf16),
            pltpu.VMEM((2, 16, 2, 32, 128), bf16),
            pltpu.VMEM((16, 2, 32, 128), bf16),
            pltpu.VMEM((2, 4, 32, 128), bf16),
            pltpu.VMEM((2, 16, 1, 128), f32),
            pltpu.VMEM((16, 1, 128), f32),
            pltpu.VMEM((2, 2, 4, 4, 2, 32, 128), bf16),
            pltpu.VMEM((2, 2, 1024, 128), f32),
            pltpu.VMEM((32, 32, 128), bf16),
            pltpu.VMEM((16, 32, 128), bf16),
            pltpu.VMEM((2, 1024, 128), bf16),
            pltpu.VMEM((2, 1024, 128), bf16),
            sem((16,)), sem((16,)), sem((16,)), sem((16,)), sem((4,)), sem((4,)), sem((4,)), sem((4,)),
            sem((8,)), sem((8,)), sem((8,)), sem((8,)), sem((1,)), sem((1,)),
            sem((16,)), sem((16,)), sem((4,)), sem((4,)), sem((16,)), sem((16,)),
            sem((2,)), sem((2,)), sem((3,)),
        ],
        compiler_params=pltpu.CompilerParams(collective_id=0, has_side_effects=True),
    )(placement, queries, grad_out, keys, values, stat_rows)
    return dq.transpose(1, 0, 2), dk[:, None, :], dv[:, None, :]


def solution(mesh):
    tokens = P(("blk", "uly"), None, None)
    return jax.shard_map(
        per_device,
        mesh=mesh,
        in_specs=(tokens,) * 5 + (P(),),
        out_specs=(tokens, P("blk", "uly", None), P("blk", "uly", None)),
        check_vma=False,
    )
```

time: 150 us -> 146 us (0.973)
  the two profiles are of different devices: /device:TPU:32 before, /device:TPU:64 now
where the time goes in v3:
time: 146 us; the launch traced here: 145 us
  Pallas kernels  139 us (95%)
  local copies, waits for them, and re-layouts  4.73 us (3%)
    pallas_call x1, Pallas kernels, per_device(): pl.pallas_call(kernel, name='exchange_grads', out_shape=(jax.ShapeDtypeSt...  139 us
    unnamed x7, local copies, waits for them, and re-layouts  3.84 us

profile of v3, /device:TPU:64, one launch (start us, length us, event | category | flops | bytes accessed | tf_op | source)
XLA Modules:
  0.0 145.4 jit_solution(13229063070932984554)
XLA Ops:
  0.6 0.7 convert_bitcast_fusion
  1.4 0.1 copy.12
  1.4 0.1 reshape.13
  1.6 0.7 tile.15.sin
  2.3 139.2 %exchange_grads.1 = (bf16[32,32,128]{2,1,0:T(8,128)(2,1)}, f32[1024,128]{1,0:T(8,128)}, f32[1024,128]{1,0:T(8,128)}) custom-call(s32[64]{0:T(128)} %place.1, bf16[32,32,128]{2,1,0:T(8,128)(2,1)} %qin.1, bf16[32,32,128]{2,1,0:T(8,128)(2,1)} %gin.1, bf16[32,4,128]{2,1,0:T(4,128)(2,1)} %kin.1, bf16[32,4,128]{2,1,0:T(4,128)(2,1)} %vin.1, f32[32,1,128]{2,1,0:T(1,128)} %tile.15.sin), custom_call_target="tpu_custom_call" | custom-call | tf_op jit(solution)/shard_map/exchange_grads/pallas_call | solution.py:273
  141.5 0.0 copy-start.1
  141.5 1.8 %copy.13 = bf16[32,32,128]{2,1,0:T(8,128)(2,1)} copy(bf16[32,32,128]{2,0,1:T(8,128)(2,1)} %bitcast.11) | data formatting | bytes 524288
  143.3 0.0 copy-done.1
  143.3 0.0 copy-start
  143.3 0.8 copy.18
  144.1 0.4 copy-done
  144.6 0.8 copy.19
  (1 shorter events, 0.0 us)
Async XLA Ops:
  141.5 1.8 %copy-start.1 = (f32[1024,128]{1,0:T(8,128)S(1)}, f32[1024,128]{1,0:T(8,128)}, u32[]{:S(2)}) copy-start(f32[1024,128]{1,0:T(8,128)} %get-tuple-element.7) | copy-start | bytes 1572868
  143.3 1.2 copy-start

commit v4 on v3

--- a/solution.py
+++ b/solution.py
@@ -16,8 +16,8 @@
 
 
 def kernel(
-    place, qin, gin, kin, vin, sin, dq_out, dk_out, dv_out,
-    qgs, inbuf, crossbuf, kvin, sinbuf, scross, kvbuf, acc, dqs, dqx, dkvs, dkvr,
+    place, qin, gin, kin, vin, stin, dq_out, dk_out, dv_out,
+    qgs, inbuf, crossbuf, kvin, sin, sinbuf, scross, kvbuf, acc, dqs, dqx, dkvs, dkvr,
     q_ss, q_rs, s_ss, s_rs, c_ss, c_rs, t_ss, t_rs, kv_ss, kv_rs, x_ss, x_rs, n_ss, n_rs,
     d_ss, d_rs, y_ss, y_rs, f_ss, f_rs, a_ss, a_rs, l_sem,
 ):
@@ -43,9 +43,16 @@
         pl.semaphore_signal(barrier, inc=1, device_id=dev, device_id_type=MESH)
     kvin[0] = kin[...].transpose(1, 0, 2)
     kvin[1] = vin[...].transpose(1, 0, 2)
-    qgs[:, 0] = qin[...].transpose(1, 0, 2)
-    qgs[:, 1] = gin[...].transpose(1, 0, 2)
-    acc[...] = jnp.zeros_like(acc)
+
+    def by_head():
+        both = stin[...].astype(f32)
+        log_norm, correction = both[:, 0, :], both[:, 1, :]
+        lanes = [log_norm, correction, log_norm, correction]
+        sin[:, 0, :] = jnp.concatenate(lanes, axis=1)
+        qgs[:, 0] = qin[...].transpose(1, 0, 2)
+        qgs[:, 1] = gin[...].transpose(1, 0, 2)
+
+    pl.when(half == 0)(by_head)
     pl.semaphore_wait(barrier, 23)
 
     def remote(src, dst, ss, rs, dev):
@@ -116,6 +123,7 @@
         kv_first(i).start()
     own_kv = pltpu.make_async_copy(kvin.at[:, row], kvbuf.at[0, :, row, col, half], l_sem.at[0])
     own_kv.start()
+    pl.when(half == 1)(by_head)
     own_qg = pltpu.make_async_copy(qgs.at[pair(0)], inbuf.at[:, 0], l_sem.at[1])
     own_qg.start()
     own_stat = pltpu.make_async_copy(sin.at[pair(0)], sinbuf.at[:, 0], l_sem.at[2])
@@ -123,6 +131,8 @@
     for r in range(1, 16):
         stat_plane(r).start()
         qg_plane(r).start()
+
+    acc[...] = jnp.zeros_like(acc)
 
     def cross(c):
         if c == 0:
@@ -205,7 +215,7 @@
 
     lax.fori_loop(1, 4, near, 0)
 
-    def distant(c, carry):
+    def distant_chunk(c):
         stat_cross(c).wait_recv()
         qg_cross(c).wait_recv()
         chunk(
@@ -213,11 +223,14 @@
             lambda j: scross[4 * c + j],
             lambda a: crossbuf[pl.ds(4 * c, 4), a],
         )
+
+    def distant(c, carry):
+        distant_chunk(c)
         dq_cross(c).start()
         return carry
 
-    lax.fori_loop(0, 4, distant, 0)
-
+    lax.fori_loop(0, 3, distant, 0)
+    distant_chunk(3)
     dkvs[0] = (acc[0, 0] * factor).astype(bf16)
     dkvs[1] = acc[0, 1].astype(bf16)
     accum = [
@@ -225,6 +238,7 @@
     ]
     for copy in accum:
         copy.start()
+    dq_cross(3).start()
     dq_cross(0).wait_recv()
     dq_out[far] = dqx[0]
     for r in (1, 2, 3):
@@ -267,7 +281,6 @@
 
 def per_device(queries, keys, values, grad_out, stats, placement):
     f32, bf16 = jnp.float32, jnp.bfloat16
-    stat_rows = jnp.tile(stats.transpose(1, 2, 0).astype(f32).reshape(32, 1, 64), (1, 1, 2))
     vmem = pl.BlockSpec(memory_space=pltpu.VMEM)
     sem = pltpu.SemaphoreType.DMA
     dq, dk, dv = pl.pallas_call(
@@ -285,6 +298,7 @@
             pltpu.VMEM((2, 16, 2, 32, 128), bf16),
             pltpu.VMEM((16, 2, 32, 128), bf16),
             pltpu.VMEM((2, 4, 32, 128), bf16),
+            pltpu.VMEM((32, 1, 128), f32),
             pltpu.VMEM((2, 16, 1, 128), f32),
             pltpu.VMEM((16, 1, 128), f32),
             pltpu.VMEM((2, 2, 4, 4, 2, 32, 128), bf16),
@@ -299,7 +313,7 @@
             sem((2,)), sem((2,)), sem((3,)),
         ],
         compiler_params=pltpu.CompilerParams(collective_id=0, has_side_effects=True),
-    )(placement, queries, grad_out, keys, values, stat_rows)
+    )(placement, queries, grad_out, keys, values, stats.transpose(1, 2, 0))
     return dq.transpose(1, 0, 2), dk[:, None, :], dv[:, None, :]
 
 

time: 146 us -> 150 us (1.027)
  the two profiles are of different devices: /device:TPU:64 before, /device:TPU:1 now
where the time goes in v4:
time: 150 us
  Pallas kernels  144 us (96%)
  local copies, waits for them, and re-layouts  5.25 us (4%)
    pallas_call x1, Pallas kernels, per_device(): pl.pallas_call(kernel, name='exchange_grads', out_shape=(jax.ShapeDtypeSt...  144 us
    unnamed x8, local copies, waits for them, and re-layouts  5.25 us

profile of v4, /device:TPU:1, one launch (start us, length us, event | category | flops | bytes accessed | tf_op | source)
XLA Modules:
  0.0 150.0 jit_solution(7283017433444703308)
XLA Ops:
  0.6 1.4 copy.9
  2.0 144.1 %exchange_grads.1 = (bf16[32,32,128]{2,1,0:T(8,128)(2,1)}, f32[1024,128]{1,0:T(8,128)}, f32[1024,128]{1,0:T(8,128)}) custom-call(s32[64]{0:T(128)} %place.1, bf16[32,32,128]{2,1,0:T(8,128)(2,1)} %qin.1, bf16[32,32,128]{2,1,0:T(8,128)(2,1)} %gin.1, bf16[32,4,128]{2,1,0:T(4,128)(2,1)} %kin.1, bf16[32,4,128]{2,1,0:T(4,128)(2,1)} %vin.1, bf16[32,2,32]{2,1,0:T(2,128)(2,1)} %bitcast.11), custom_call_target="tpu_custom_call" | custom-call | tf_op jit(solution)/shard_map/exchange_grads/pallas_call | solution.py:286
  146.2 0.0 copy-start.1
  146.2 1.8 %copy.10 = bf16[32,32,128]{2,1,0:T(8,128)(2,1)} copy(bf16[32,32,128]{2,0,1:T(8,128)(2,1)} %bitcast.10) | data formatting | bytes 524288
  148.0 0.0 copy-done.1
  148.0 0.0 copy-start
  148.0 0.8 copy.15
  148.8 0.4 copy-done
  149.2 0.8 copy.16
Async XLA Ops:
  146.2 1.8 %copy-start.1 = (f32[1024,128]{1,0:T(8,128)S(1)}, f32[1024,128]{1,0:T(8,128)}, u32[]{:S(2)}) copy-start(f32[1024,128]{1,0:T(8,128)} %get-tuple-element.7) | copy-start | bytes 1572868
  148.0 1.2 copy-start
